TPU v7x, 512 devices: a whole 4x8x8 slice. The times are simulated.
512 devices in a mesh: section: 16 (over z_lo, y), shard: 32 (over x, z_hi, core).
Axes of the slice: x: 4, y: 8, z: 8 (z_hi: 4, z_lo: 2; z = z_hi * 2 + z_lo), core: 2. Of those that a mesh axis runs over, the one named last changes fastest.
Arguments:
- layer_input: bfloat16 [16, 4096, 3072], P('section', 'shard'), may hold values from -150 to 150
- out_grad: bfloat16 [16, 4096, 3072], P('section', 'shard'), may hold values from -60 to 60
- modulation: float32 [16, 4, 3, 3072], P('section'), may hold values from -3 to 3
- proj_weight: bfloat16 [16, 3072, 3072], P('section', 'shard'), may hold values from -0.109375 to 0.109375
Outputs:
- handoff: bfloat16 [16, 4096, 3072], P('section', 'shard')
- mod_grad: float32 [16, 4, 3, 3072], P('section')
All inputs are finite; a program needn't handle non-finite values.
Results may differ from a plain program's by a relative error of at most 0.0029.
Values may be sent and summed in bfloat16 or wider, within the bound.
A program may use at most 128 MiB of HBM per device.

v0:
```python
import jax
import jax.numpy as jnp
from jax import lax
from jax.sharding import PartitionSpec as P

SEQS = 4


def swapped(value, axis, apart):
    mask = 2**apart
    pairs = [(source, source ^ mask) for source in range(lax.axis_size(axis))]
    return lax.ppermute(value, axis, pairs)


def passed_along(value, axis, steps):
    count = lax.axis_size(axis)
    leading, last = (max(0, -steps), min(count, count - steps))
    return lax.ppermute(value, axis, [(source, source + steps) for source in range(leading, last)])


def select_rows(token_ids, seq_length):
    sample = token_ids // seq_length
    return (sample[:, None] == jnp.arange(SEQS, dtype=jnp.int32)[None, :]).astype(jnp.float32)


def norm_rows(activation):
    values = activation.astype(jnp.float32)
    center = values - jnp.mean(values, axis=-1, keepdims=True)
    variance = jnp.mean(center * center, axis=-1, keepdims=True)
    inv_scale = lax.rsqrt(variance + 1e-06)
    return (center * inv_scale, inv_scale)


def on_device(layer_input, out_grad, modulation, proj_weight):
    shard_count = lax.axis_size("shard")
    my_index = lax.axis_index("shard")
    group_bits = 1
    group_size = 2**group_bits
    own_input = layer_input[0]
    own_grad = out_grad[0]
    mod_table = modulation[0]
    weight_rows = proj_weight[0]
    row_count, feat_count = own_input.shape
    col_count = feat_count // group_size
    seq_length = row_count * shard_count // SEQS
    position = my_index % group_size
    own_sample = my_index * row_count // seq_length
    own_mod = lax.dynamic_index_in_dim(mod_table, own_sample, 0, keepdims=False)
    sample_hot = (jnp.arange(SEQS, dtype=jnp.int32) == own_sample).astype(jnp.float32)
    normed, inv_scale = norm_rows(own_input)
    modulated = (normed * (1.0 + own_mod[1]) + own_mod[0]).astype(jnp.bfloat16)
    joined = jnp.stack([modulated, own_grad], axis=0)
    bit_number = 0
    partner = swapped(joined, "shard", bit_number)
    upper_side = my_index // 2**bit_number % 2 == 1
    lower_part = jnp.where(upper_side, partner, joined)
    upper_part = jnp.where(upper_side, joined, partner)
    joined = jnp.concatenate([lower_part, upper_part], axis=1)
    group_input = joined[0]
    group_grad = joined[1]
    piece_rows = weight_rows.shape[0]
    pieces = jnp.transpose(weight_rows.reshape(piece_rows, group_size, col_count), (1, 0, 2))
    outgoing = jnp.broadcast_to(
        pieces[None], (shard_count // group_size, group_size, piece_rows, col_count)
    )
    outgoing = outgoing.reshape(shard_count, piece_rows, col_count)
    incoming = lax.all_to_all(outgoing, "shard", split_axis=0, concat_axis=0, tiled=True)
    weight_cols = incoming.reshape(feat_count, col_count)
    group_ids = (my_index - position) * row_count + jnp.arange(
        group_size * row_count, dtype=jnp.int32
    )
    group_select = select_rows(group_ids, seq_length)
    col_start = position * col_count
    gate_table = lax.dynamic_slice_in_dim(mod_table[:, 2], col_start, col_count, 1)
    gate_cols = jnp.dot(group_select, gate_table, precision=lax.Precision.HIGHEST)
    grad_cols = lax.dynamic_slice_in_dim(group_grad, col_start, col_count, 1).astype(jnp.float32)
    branch = jnp.dot(group_input, weight_cols, preferred_element_type=jnp.float32)
    scaled_grad = (gate_cols * grad_cols).astype(jnp.bfloat16)
    partial_grad = lax.dot_general(
        scaled_grad, weight_cols, (((1,), (1,)), ((), ())), preferred_element_type=jnp.float32
    )
    gate_part = jnp.einsum(
        "rs,rd->sd", group_select, grad_cols * branch, precision=lax.Precision.HIGHEST
    )
    gate_full = lax.dynamic_update_slice(
        jnp.zeros((SEQS, feat_count), jnp.float32), gate_part, (jnp.int32(0), col_start)
    )
    current = partial_grad
    for bit_number in reversed(range(group_bits)):
        half_count = current.shape[0] // 2
        low_half = current[:half_count]
        high_half = current[half_count:]
        upper_side = my_index // 2**bit_number % 2 == 1
        kept_half = jnp.where(upper_side, high_half, low_half)
        sending = jnp.where(upper_side, low_half, high_half)
        current = kept_half + swapped(sending.astype(jnp.bfloat16), "shard", bit_number).astype(
            sending.dtype
        )
    grad_shift = sample_hot[:, None] * jnp.sum(current, axis=0)[None, :]
    grad_scale = sample_hot[:, None] * jnp.sum(current * normed, axis=0)[None, :]
    totals = lax.psum(jnp.stack([grad_shift, grad_scale, gate_full], axis=1), "shard")
    grad_norm = current * (1.0 + own_mod[1])
    centered = grad_norm - jnp.mean(grad_norm, axis=-1, keepdims=True)
    grad_in = own_grad.astype(jnp.float32) + inv_scale * (
        centered - normed * jnp.mean(grad_norm * normed, axis=-1, keepdims=True)
    )
    handoff = passed_along(grad_in.astype(jnp.bfloat16), "section", -1)
    return (handoff[None], totals[None])


def solution(mesh):
    in_specs = (
        P("section", "shard", None),
        P("section", "shard", None),
        P("section", None, None, None),
        P("section", "shard", None),
    )
    out_specs = (P("section", "shard", None), P("section", None, None, None))
    return jax.shard_map(
        on_device, mesh=mesh, in_specs=in_specs, out_specs=out_specs, check_vma=False
    )
```

profile of v0, /device:TPU:57, one launch (start us, length us, event | category | flops | bytes accessed | tf_op | source)
XLA Modules:
  0.0 537.1 jit_solution(8000382200679305160)
XLA Ops:
  7.2 2.2 reshape_squeeze.3
  9.4 0.1 copy.6
  9.4 4.7 broadcast_in_dim.8
  14.2 0.0 copy-start
  14.2 13.8 %all-to-all-start = ((bf16[32,96,1536]{2,1,0:T(8,128)(2,1)}), bf16[32,96,1536]{2,1,0:T(8,128)(2,1)}, u32[]{:S(2)}, u32[]{:S(2)}) async-start(bf16[32,96,1536]{2,1,0:T(8,128)(2,1)} %bitcast.61), calls=%async_computation | async-start | bytes 18874368 | tf_op jit(solution)/shard_map/all_to_all | solution.py:67
  27.9 0.0 copy-start.9
  27.9 0.0 all-reduce.2.cloned.1.call-start
  28.0 0.0 copy-done
  28.0 0.0 copy-start.1
  28.0 0.2 convert_reduce_fusion
  28.2 0.4 fusion.14
  28.6 0.2 copy-done.9
  28.9 0.4 fusion.18
  29.3 0.0 copy-done.1
  29.3 1.3 pad_maximum_fusion.1
  30.6 2.2 collective-permute-start
  32.9 3.4 collective-permute-done
  36.2 1.6 broadcast_select_fusion.1
  37.8 0.0 copy-start.2
  37.8 0.0 copy-start.4
  37.9 0.3 pad_slice_fusion
  38.2 0.8 copy-done.2
  39.0 0.5 copy-done.4
  39.5 0.0 copy-start.6
  39.5 1.2 copy-done.6
  40.7 1.8 fusion
  42.5 144.0 %all-to-all-done = bf16[32,96,1536]{2,1,0:T(8,128)(2,1)} async-done(((bf16[32,96,1536]{2,1,0:T(8,128)(2,1)}), bf16[32,96,1536]{2,1,0:T(8,128)(2,1)}, u32[]{:S(2)}, u32[]{:S(2)}) %all-to-all-start) | async-done | bytes 9437216 | tf_op jit(solution)/shard_map/all_to_all | solution.py:67
  186.5 5.6 %fusion.29 = f32[256,3072]{1,0:T(8,128)S(1)} fusion(bf16[256,1536]{1,0:T(8,128)(2,1)} %fusion, bf16[3072,1536]{1,0:T(8,128)(2,1)} %bitcast.9), kind=kOutput, calls=%fused_computation.59 | convolution fusion | flops 2415919104 | bytes 13369344 | tf_op jit(solution)/shard_map/dot_general | solution.py:79
  192.1 0.0 copy-start.3
  192.1 0.1 select_convert_fusion
  192.3 3.7 collective-permute-start.1
  196.0 0.0 copy-done.5
  196.0 0.0 copy-done.7
  196.0 0.0 copy-done.3
  196.1 5.2 convolution_multiply_fusion
  201.3 0.7 fusion.1
  202.0 0.0 collective-permute-done.1
  202.0 1.0 fusion.13
  203.0 0.8 fusion.12
  203.7 3.0 collective-permute-start.2
  206.7 0.1 broadcast_multiply_fusion.1
  206.8 0.7 maximum_bitcast_fusion
  207.5 0.0 all-reduce.2.cloned.1.call-update
  207.5 70.1 %collective-permute-done.2 = bf16[128,3072]{1,0:T(8,128)(2,1)S(1)} collective-permute-done((bf16[128,3072]{1,0:T(8,128)(2,1)S(1)}, bf16[128,3072]{1,0:T(8,128)(2,1)S(1)}, u32[]{:S(2)}, u32[]{:S(2)}) %collective-permute-start.2) | collective-permute-done | bytes 786464 | tf_op jit(solution)/shard_map/ppermute | solution.py:18
  277.6 250.9 %all-reduce.2.cloned.1.call-done = f32[1,4,3,3072]{3,1,2,0:T(4,128)} async-done(((f32[1,4,3,3072]{3,1,2,0:T(4,128)}), f32[1,4,3,3072]{3,1,2,0:T(4,128)}) %all-reduce.2.cloned.1.call-update) | async-done | bytes 147472 | tf_op jit(solution)/shard_map/psum | solution.py:101
  528.5 0.9 copy.10
  529.4 0.1 copy-done.8
  529.6 0.7 copy.11
  (12 shorter events, 0.1 us)
Async XLA Ops:
  14.2 13.9 %copy-start = (bf16[1,128,3072]{2,1,0:T(8,128)(2,1)S(1)}, bf16[1,128,3072]{2,1,0:T(8,128)(2,1)}, u32[]{:S(2)}) copy-start(bf16[1,128,3072]{2,1,0:T(8,128)(2,1)} %param.4) | copy-start | bytes 2359300
  14.2 172.4 %all-to-all-start = ((bf16[32,96,1536]{2,1,0:T(8,128)(2,1)}), bf16[32,96,1536]{2,1,0:T(8,128)(2,1)}, u32[]{:S(2)}, u32[]{:S(2)}) async-start(bf16[32,96,1536]{2,1,0:T(8,128)(2,1)} %bitcast.61), calls=%async_computation | async-start | bytes 18874368 | tf_op jit(solution)/shard_map/all_to_all | solution.py:67
  27.9 0.9 copy-start.9
  27.9 500.6 %all-reduce.2.cloned.1.call-start = ((), (), s32[]{:S(2)}) async-start(), calls=%async_computation.1 | async-start | bytes 294912 | tf_op jit(solution)/shard_map/psum | solution.py:101
  28.0 1.2 copy-start.1
  30.6 5.6 %collective-permute-start = (bf16[2,128,3072]{2,1,0:T(8,128)(2,1)}, bf16[2,128,3072]{2,1,0:T(8,128)(2,1)}, u32[]{:S(2)}, u32[]{:S(2)}) collective-permute-start(bf16[2,128,3072]{2,1,0:T(8,128)(2,1)} %pad_maximum_fusion.1), channel_id=1, source_target_pairs={{0,1},{1,0},{2,3},{3,2},{4,5},{5,4},{6,7},{7,6},{8,9},{9,8},{10,11... | collective-permute-start | bytes 4718600 | tf_op jit(solution)/shard_map/ppermute | solution.py:12
  37.8 1.2 copy-start.2
  37.8 1.7 copy-start.4
  39.5 1.2 copy-start.6
  186.5 9.5 %copy-start.5 = (bf16[2,128,3072]{2,1,0:T(8,128)(2,1)S(1)}, bf16[2,128,3072]{2,1,0:T(8,128)(2,1)}, u32[]{:S(2)}) copy-start(bf16[2,128,3072]{2,1,0:T(8,128)(2,1)} %copy-done.4) | copy-start | bytes 4718596
  186.5 9.5 %copy-start.7 = (bf16[1,256,3072]{2,1,0:T(8,128)(2,1)S(1)}, bf16[1,256,3072]{2,1,0:T(8,128)(2,1)}, u32[]{:S(2)}) copy-start(bf16[1,256,3072]{2,1,0:T(8,128)(2,1)} %copy-done.6) | copy-start | bytes 4718596
  192.1 3.9 copy-start.3
  192.3 9.7 %collective-permute-start.1 = (bf16[128,3072]{1,0:T(8,128)(2,1)S(1)}, bf16[128,3072]{1,0:T(8,128)(2,1)S(1)}, u32[]{:S(2)}, u32[]{:S(2)}) collective-permute-start(bf16[128,3072]{1,0:T(8,128)(2,1)S(1)} %select_convert_fusion), channel_id=1, source_target_pairs={{0,1},{1,0},{2,3},{3,2},{4,5},{5,4},{6,7},{7,6},{8,9},{9,8},{10,11... | collective-permute-start | bytes 2359304 | tf_op jit(solution)/shard_map/ppermute | solution.py:12
  203.7 73.9 %collective-permute-start.2 = (bf16[128,3072]{1,0:T(8,128)(2,1)S(1)}, bf16[128,3072]{1,0:T(8,128)(2,1)S(1)}, u32[]{:S(2)}, u32[]{:S(2)}) collective-permute-start(bf16[128,3072]{1,0:T(8,128)(2,1)S(1)} %fusion.12), channel_id=1, source_target_pairs={{32,0},{64,32},{96,64},{128,96},{160,128},{192,160},{224,192},{256... | collective-permute-start | bytes 2359304 | tf_op jit(solution)/shard_map/ppermute | solution.py:18
  528.5 1.0 copy-start.8
Sparse Core Ops, SparseCore 0:
  207.6 320.8 all-reduce.1
where the time goes:
time: 539 us; the launch traced here: 537 us
  waiting for transfers between devices  468 us (87%)
  starting transfers between devices  22.7 us (4%)
  between operations  14.3 us (3%)
  matrix products  13.3 us (2%)
  local copies, waits for them, and re-layouts  11.8 us (2%)
  other arithmetic  6.55 us (1%)
    psum x1, waiting for transfers between devices, on_device(): lax.psum(jnp.stack([grad_shift, grad_scale, gate_full], axis=1), 'shard')  251 us
    all_to_all x1, waiting for transfers between devices, on_device(): lax.all_to_all(outgoing, 'shard', split_axis=0, concat_axis=0, tiled=True)  144 us
    ppermute x1, waiting for transfers between devices, passed_along(): lax.ppermute(value, axis, [(source, source + steps) for source in range(l...  70.1 us
    all_to_all x1, starting transfers between devices, on_device(): lax.all_to_all(outgoing, 'shard', split_axis=0, concat_axis=0, tiled=True)  13.8 us
  transfers between devices with their start and end apart: 5, of which 4 were waited for; matrix products, arithmetic and copies ran while one was open for 2% of the time, Pallas kernels for 0%

commit v1 on v0

v1 whole, which is shorter than its diff:
```python
import functools

import jax
import jax.numpy as jnp
from jax import lax
from jax.experimental import pallas as pl
from jax.experimental.pallas import tpu as pltpu
from jax.sharding import PartitionSpec as P

MESH = pl.DeviceIdType.MESH
F32 = jnp.float32
BF16 = jnp.bfloat16

SEQS = 4
OFF = (0, 3, 1, 2)
AWAY = (0, 1, 3, 2)
LANES = 128
COPIES = 64


def stats_to_rows(first, second):
    lane = lax.broadcasted_iota(jnp.int32, (LANES, LANES), 1)
    square = jnp.where(lane == 0, first, jnp.where(lane == 1, second, 0.0))
    return jnp.transpose(square)[:8]


def rows_to_stats(rows):
    square = jnp.concatenate([rows, jnp.zeros((LANES - 8, LANES), F32)], axis=0)
    columns = jnp.transpose(square)
    return columns[:, 0:1], columns[:, 1:2]


def kernel(
    sections, li_ref, og_ref, mod_ref, w_ref, out_ref, mg_ref,
    og_all, li_all, w_all, st_all, scaled, normed, inv_all, modulated, gm, gn, outgoing,
    gate_acc, sums, part, gate_buf, gate_rx, rs, full, send_sem, recv_sem, local_sem,
):
    rows, feats = og_ref.shape
    block = feats // 4
    chunk = feats // 16
    w_rows = w_ref.shape[0]
    owners = block // LANES
    half, w_half = rows // 2, w_rows // 2

    sec = lax.axis_index("section")
    shard = lax.axis_index("shard")
    x = shard // 8
    z = (shard % 8) // 2
    c = shard % 2
    other = 1 - c

    def at_x(k):
        return (sec, lax.rem(x + k, 4) * 8 + z * 2 + c)

    def at_z(dz, dc):
        return (sec, x * 8 + lax.rem(z + dz, 4) * 2 + lax.rem(c + dc, 2))

    def at_section(step, pos):
        return (sec + step, pos * 8 + z * 2 + c)

    def copy(ident, src, dst, device):
        return pltpu.make_async_remote_copy(
            src_ref=src, dst_ref=dst, send_sem=send_sem.at[ident], recv_sem=recv_sem.at[ident],
            device_id=device, device_id_type=MESH,
        )

    ids = iter(range(COPIES))
    slot_x = [lax.rem(x + OFF[n], 4) for n in range(4)]
    group = [(dz, dc) for dz in range(4) for dc in range(2) if (dz, dc) != (0, 0)]

    def columns(pos):
        return pl.ds(pl.multiple_of(pos * block, LANES), block)

    own_columns = columns(x)

    barrier = pltpu.get_barrier_semaphore()

    def greet(device):
        pl.semaphore_signal(barrier, inc=1, device_id=device, device_id_type=MESH)

    for k in range(1, 4):
        greet(at_x(k))
    for dz, dc in group:
        greet(at_z(dz, dc))

    @pl.when(sec > 0)
    def _():
        for pos in range(4):
            greet(at_section(-1, pos))

    @pl.when(sec < sections - 1)
    def _():
        for pos in range(4):
            greet(at_section(1, pos))

    neighbours = (sec + sections - 1) // sections + (2 * sections - 2 - sec) // sections
    pl.semaphore_wait(barrier, 3 + len(group) + 4 * neighbours)

    low, high = pl.ds(0, half), pl.ds(half, half)
    w_low, w_high = pl.ds(0, w_half), pl.ds(w_half, w_half)
    og_r_low = copy(next(ids), og_ref.at[low], og_all.at[1, low], at_x(1))
    og_r_high = copy(next(ids), og_ref.at[high], og_all.at[1, high], at_x(1))
    og_l_high = copy(next(ids), og_ref.at[high], og_all.at[2, high], at_x(3))
    og_l_low = copy(next(ids), og_ref.at[low], og_all.at[2, low], at_x(3))
    og_fr = copy(next(ids), og_all.at[1, low], og_all.at[3, low], at_x(1))
    og_fl = copy(next(ids), og_all.at[2, high], og_all.at[3, high], at_x(3))
    w_u_low = copy(next(ids), w_ref.at[w_low], w_all.at[1, c, w_low], at_z(1, 0))
    w_u_high = copy(next(ids), w_ref.at[w_high], w_all.at[1, c, w_high], at_z(1, 0))
    w_d_high = copy(next(ids), w_ref.at[w_high], w_all.at[2, c, w_high], at_z(3, 0))
    w_d_low = copy(next(ids), w_ref.at[w_low], w_all.at[2, c, w_low], at_z(3, 0))
    w_fu = copy(next(ids), w_all.at[1, c, w_low], w_all.at[3, c, w_low], at_z(1, 0))
    w_fd = copy(next(ids), w_all.at[2, c, w_high], w_all.at[3, c, w_high], at_z(3, 0))
    li_sends = [
        copy(next(ids), li_ref.at[:, columns(lax.rem(x + AWAY[n], 4))], li_all.at[n], at_x(AWAY[n]))
        for n in (1, 2, 3)
    ]
    st_sends = [copy(next(ids), st_all.at[0], st_all.at[n], at_x(AWAY[n])) for n in (1, 2, 3)]
    own_sib = next(ids)
    w_sib = copy(own_sib, w_ref, w_all.at[0, c], at_z(0, 1))
    w_sib_in = copy(own_sib, w_ref, w_all.at[0, other], at_z(0, 1))

    for step in (og_r_low, og_l_high, w_u_low, w_d_high, og_r_high, og_l_low, w_u_high, w_d_low, w_sib):
        step.start()
    for step in li_sends:
        step.start()
    local = [
        pltpu.make_async_copy(og_ref, og_all.at[0], local_sem.at[0]),
        pltpu.make_async_copy(li_ref.at[:, own_columns], li_all.at[0], local_sem.at[1]),
        pltpu.make_async_copy(w_ref, w_all.at[0, c], local_sem.at[2]),
    ]
    for step in local:
        step.start()

    sib_sends, sib_waits = [w_sib], {}

    def to_sibling(slot, part_rows):
        ident = next(ids)
        place = w_all.at[slot, c, part_rows]
        send = copy(ident, place, place, at_z(0, 1))
        send.start()
        sib_sends.append(send)
        sib_waits.setdefault(slot, []).append(copy(ident, place, w_all.at[slot, other, part_rows], at_z(0, 1)))

    values = li_ref[...].astype(F32)
    mean = jnp.sum(values, axis=1, keepdims=True) / feats
    center = values - mean
    variance = jnp.sum(center * center, axis=1, keepdims=True) / feats
    st_all[0] = stats_to_rows(mean, lax.rsqrt(variance + 1e-06))
    for step in st_sends:
        step.start()
    gate_acc[...] = jnp.zeros_like(gate_acc)
    for step in local:
        step.wait()

    def scale_grad(n):
        gate = mod_ref[2, pl.ds(slot_x[n], 1), :]
        scaled[n] = (gate * og_all[n].astype(F32)).astype(BF16)

    def modulate(n):
        mean_n, inv_n = rows_to_stats(st_all[n])
        inv_all[n] = inv_n
        norm_n = (li_all[n].astype(F32) - mean_n) * inv_n
        normed[n] = norm_n
        scale = mod_ref[1, pl.ds(slot_x[n], 1), own_columns]
        shift = mod_ref[0, pl.ds(slot_x[n], 1), own_columns]
        mod_n = (norm_n * (1.0 + scale) + shift).astype(BF16)
        for j in range(4):
            modulated[j, n] = mod_n[:, j * chunk:(j + 1) * chunk]

    scale_grad(0)
    modulate(0)

    og_r_low.wait_recv()
    og_fr.start()
    og_l_high.wait_recv()
    og_fl.start()
    w_u_low.wait_recv()
    w_fu.start()
    to_sibling(1, w_low)
    w_d_high.wait_recv()
    w_fd.start()
    to_sibling(2, w_high)
    og_r_high.wait_recv()
    og_l_low.wait_recv()
    scale_grad(1)
    scale_grad(2)
    for n in (1, 2):
        li_sends[n - 1].wait_recv()
        st_sends[n - 1].wait_recv()
        modulate(n)
    w_u_high.wait_recv()
    to_sibling(1, w_high)
    w_d_low.wait_recv()
    to_sibling(2, w_low)
    w_sib_in.wait_recv()
    for slot in (1, 2):
        for step in sib_waits[slot]:
            step.wait_recv()

    tile = 512

    def chunk_of(slot):
        return lax.rem(z + jnp.where(slot == 1, 3, jnp.where(slot == 2, 1, jnp.where(slot == 3, 2, 0))), 4)

    def grad_product(slot, first, count):
        j = chunk_of(slot)
        left = scaled[first:first + count].reshape(count * rows, feats)
        right = w_all[slot].reshape(chunk, feats)
        product = lax.dot_general(left, right, (((1,), (1,)), ((), ())), preferred_element_type=F32)
        gm[j, first:first + count] = product.reshape(count, rows, chunk)

    def branch_product(slot, first, count):
        j = chunk_of(slot)

        def body(step, carry):
            cols = pl.ds(pl.multiple_of(step * tile, tile), tile)
            left = modulated[j, first:first + count].reshape(count * rows, chunk)
            right = w_all[slot, :, :, cols].reshape(chunk, tile)
            branch = jnp.dot(left, right, preferred_element_type=F32)
            weighed = branch.reshape(count, rows, tile) * og_all[first:first + count, :, cols].astype(F32)
            gate_acc[first:first + count, :, cols] += jnp.sum(
                weighed.reshape(count, rows // 8, 8, tile), axis=1
            )
            return carry

        lax.fori_loop(0, feats // tile, body, 0)

    def early(first, count):
        def body(slot, carry):
            grad_product(slot, first, count)
            branch_product(slot, first, count)
            return carry

        lax.fori_loop(0, 3, body, 0)

    early(0, 3)

    og_fr.wait_recv()
    og_fl.wait_recv()
    scale_grad(3)
    li_sends[2].wait_recv()
    st_sends[2].wait_recv()
    modulate(3)
    early(3, 1)

    w_fu.wait_recv()
    to_sibling(3, w_low)
    w_fd.wait_recv()
    to_sibling(3, w_high)
    for step in sib_waits[3]:
        step.wait_recv()
    grad_product(3, 0, 4)

    def joined(n):
        return jnp.concatenate([gm[j, n] for j in range(4)], axis=1)

    for n in range(4):
        scale = mod_ref[1, pl.ds(slot_x[n], 1), own_columns]
        grad_norm = joined(n) * (1.0 + scale)
        gn[n] = grad_norm
        sums[0, slot_x[n]] = stats_to_rows(
            jnp.sum(grad_norm, axis=1, keepdims=True),
            jnp.sum(grad_norm * normed[n], axis=1, keepdims=True),
        )
    sum_sends = [copy(next(ids), sums.at[0], sums.at[n], at_x(AWAY[n])) for n in (1, 2, 3)]
    for step in sum_sends:
        step.start()

    def place_rows(per_slot):
        row = lax.broadcasted_iota(jnp.int32, (SEQS, per_slot[0].shape[1]), 0)
        total = jnp.zeros(row.shape, F32)
        for n in range(4):
            total = total + jnp.where(row == slot_x[n], per_slot[n], 0.0)
        return total

    shifts, scales = [], []
    for n in range(4):
        grad_mod = joined(n)
        shifts.append(jnp.sum(grad_mod, axis=0, keepdims=True))
        scales.append(jnp.sum(grad_mod * normed[n], axis=0, keepdims=True))
    part[0] = place_rows(shifts)
    part[1] = place_rows(scales)

    for step in sum_sends:
        step.wait_recv()
    hand_ids = [next(ids) for n in range(4)]

    def hand(n):
        return copy(hand_ids[n], outgoing.at[n], out_ref.at[:, own_columns], at_section(-1, slot_x[n]))

    for n in range(4):
        rows_of = sums[0, slot_x[n]] + sums[1, slot_x[n]] + sums[2, slot_x[n]] + sums[3, slot_x[n]]
        first, second = rows_to_stats(rows_of)
        centered = gn[n] - first / feats
        grad_in = og_all[n, :, own_columns].astype(F32) + inv_all[n] * (centered - normed[n] * (second / feats))
        outgoing[n] = grad_in.astype(BF16)

        @pl.when(sec > 0)
        def _(n=n):
            hand(n).start()

    @pl.when(sec == sections - 1)
    def _():
        out_ref[...] = jnp.zeros_like(out_ref)

    branch_product(3, 0, 4)

    gate_buf[...] = place_rows([jnp.sum(gate_acc[n], axis=0, keepdims=True) for n in range(4)])
    gate_sends = [
        copy(next(ids), gate_buf.at[:, columns(lax.rem(x + AWAY[n], 4))], gate_rx.at[n - 1], at_x(AWAY[n]))
        for n in (1, 2, 3)
    ]
    for step in gate_sends:
        step.start()
    for step in gate_sends:
        step.wait_recv()
    part[2] = gate_buf[:, own_columns] + gate_rx[0] + gate_rx[1] + gate_rx[2]

    def owned(owner):
        return pl.ds(pl.multiple_of(owner * LANES, LANES), LANES)

    owns = z < owners // 2
    me = z * 2 + c
    rs_ids = [next(ids) for _ in group]
    ag_ids = [next(ids) for _ in group]

    def rs_copy(i):
        dz, dc = group[i]
        owner = lax.rem(z + dz, 4) * 2 + lax.rem(c + dc, 2)
        return copy(rs_ids[i], part.at[:, :, owned(owner)], rs.at[i], at_z(dz, dc))

    def gives(i):
        return lax.rem(z + group[i][0], 4) < owners // 2

    for i in range(len(group)):
        @pl.when(gives(i))
        def _(i=i):
            rs_copy(i).start()

    @pl.when(owns)
    def _():
        total = part[:, :, owned(me)]
        for i in range(len(group)):
            dz, dc = group[i]
            copy(rs_ids[i], rs.at[i], rs.at[i], at_z(dz, dc)).wait_recv()
        for i in range(len(group)):
            total = total + rs[i]
        full[0, me] = total
        for i in range(len(group)):
            dz, dc = group[i]
            copy(ag_ids[i], full.at[0, me], full.at[0, me], at_z(dz, dc)).start()

    for i in range(len(group)):
        dz, dc = group[i]
        from_z = lax.rem(z + 4 - dz, 4)
        source = from_z * 2 + lax.rem(c + dc, 2)

        @pl.when(from_z < owners // 2)
        def _(i=i, source=source, dz=dz, dc=dc):
            landed = full.at[0, source]
            copy(ag_ids[i], landed, landed, at_z(dz, dc)).wait_recv()

    full_sends = [copy(next(ids), full.at[0], full.at[n], at_x(AWAY[n])) for n in (1, 2, 3)]
    for step in full_sends:
        step.start()
    for step in full_sends:
        step.wait_recv()
    for n in range(4):
        for owner in range(owners):
            start = pl.multiple_of(slot_x[n] * block + owner * LANES, LANES)
            mg_ref[:, :, pl.ds(start, LANES)] = full[n, owner]

    for step in (
        og_r_low, og_r_high, og_l_high, og_l_low, og_fr, og_fl, w_u_low, w_u_high, w_d_high, w_d_low,
        w_fu, w_fd, *li_sends, *st_sends, *sib_sends, *sum_sends, *gate_sends, *full_sends,
    ):
        step.wait_send()
    for i in range(len(group)):
        @pl.when(gives(i))
        def _(i=i):
            rs_copy(i).wait_send()

    @pl.when(owns)
    def _():
        for i in range(len(group)):
            dz, dc = group[i]
            copy(ag_ids[i], full.at[0, me], full.at[0, me], at_z(dz, dc)).wait_send()

    @pl.when(sec > 0)
    def _():
        for n in range(4):
            hand(n).wait_send()

    @pl.when(sec < sections - 1)
    def _():
        for n in range(4):
            landed = out_ref.at[:, columns(lax.rem(x + 4 - OFF[n], 4))]
            copy(hand_ids[n], outgoing.at[n], landed, at_section(1, slot_x[n])).wait_recv()


def on_device(layer_input, out_grad, modulation, proj_weight):
    sections = lax.axis_size("section")
    rows, feats = layer_input.shape[1:]
    w_rows = proj_weight.shape[1]
    block, chunk = feats // 4, feats // 16
    owners = block // LANES
    vmem = pl.BlockSpec(memory_space=pltpu.VMEM)
    handoff, grads = pl.pallas_call(
        functools.partial(kernel, sections),
        out_shape=(
            jax.ShapeDtypeStruct((rows, feats), BF16),
            jax.ShapeDtypeStruct((3, SEQS, feats), F32),
        ),
        in_specs=[vmem] * 4,
        out_specs=(vmem, vmem),
        scratch_shapes=[
            pltpu.VMEM((4, rows, feats), BF16),
            pltpu.VMEM((4, rows, block), BF16),
            pltpu.VMEM((4, 2, w_rows, feats), BF16),
            pltpu.VMEM((4, 8, LANES), F32),
            pltpu.VMEM((4, rows, feats), BF16),
            pltpu.VMEM((4, rows, block), F32),
            pltpu.VMEM((4, rows, 1), F32),
            pltpu.VMEM((4, 4, rows, chunk), BF16),
            pltpu.VMEM((4, 4, rows, chunk), F32),
            pltpu.VMEM((4, rows, block), F32),
            pltpu.VMEM((4, rows, block), BF16),
            pltpu.VMEM((4, 8, feats), F32),
            pltpu.VMEM((4, 4, 8, LANES), F32),
            pltpu.VMEM((3, SEQS, block), F32),
            pltpu.VMEM((SEQS, feats), F32),
            pltpu.VMEM((3, SEQS, block), F32),
            pltpu.VMEM((7, 3, SEQS, LANES), F32),
            pltpu.VMEM((4, owners, 3, SEQS, LANES), F32),
            pltpu.SemaphoreType.DMA((COPIES,)),
            pltpu.SemaphoreType.DMA((COPIES,)),
            pltpu.SemaphoreType.DMA((3,)),
        ],
        compiler_params=pltpu.CompilerParams(
            collective_id=0, has_side_effects=True, vmem_limit_bytes=56 * 1024 * 1024
        ),
    )(layer_input[0], out_grad[0], jnp.transpose(modulation[0], (1, 0, 2)), proj_weight[0])
    return (handoff[None], jnp.transpose(grads, (1, 0, 2))[None])


def solution(mesh):
    in_specs = (
        P("section", "shard", None),
        P("section", "shard", None),
        P("section", None, None, None),
        P("section", "shard", None),
    )
    out_specs = (P("section", "shard", None), P("section", None, None, None))
    return jax.shard_map(
        on_device, mesh=mesh, in_specs=in_specs, out_specs=out_specs, check_vma=False
    )
```

time: 539 us -> 103 us (0.19)
  the two profiles are of different devices: /device:TPU:57 before, /device:TPU:120 now
where the time goes in v1:
time: 103 us
  Pallas kernels  99.2 us (96%)
  local copies, waits for them, and re-layouts  2.76 us (3%)
    pallas_call x1, Pallas kernels, on_device(): pl.pallas_call(functools.partial(kernel, sections), out_shape=(jax.ShapeD...  99.2 us
    unnamed x4, local copies, waits for them, and re-layouts  2.76 us

profile of v1, /device:TPU:120, one launch (start us, length us, event | category | flops | bytes accessed | tf_op | source)
XLA Modules:
  0.0 102.6 jit_solution(7820593933480763073)
XLA Ops:
  0.6 99.2 %shard_map.59 = (bf16[128,3072]{1,0:T(8,128)(2,1)}, f32[3,4,3072]{2,1,0:T(4,128)}) custom-call(bf16[128,3072]{1,0:T(8,128)(2,1)} %bitcast.11, bf16[128,3072]{1,0:T(8,128)(2,1)} %bitcast.12, f32[3,4,3072]{2,1,0:T(4,128)} %bitcast.14, bf16[96,3072]{1,0:T(8,128)(2,1)} %bitcast.13), custom_call_target="tpu_custom_call" | custom-call | tf_op jit(solution)/shard_map/pallas_call | solution.py:408
  99.8 0.0 copy-start
  99.8 2.1 %copy.8 = bf16[1,128,3072]{2,1,0:T(8,128)(2,1)} copy(bf16[1,128,3072]{2,1,0:T(8,128)(2,1)} %bitcast.10) | data formatting | bytes 1572864
  101.9 0.0 copy-done
  101.9 0.7 copy.9
Async XLA Ops:
  99.8 2.1 %copy-start = (f32[3,4,3072]{2,1,0:T(4,128)S(1)}, f32[3,4,3072]{2,1,0:T(4,128)}, u32[]{:S(2)}) copy-start(f32[3,4,3072]{2,1,0:T(4,128)} %get-tuple-element.5) | copy-start | bytes 442372

commit v2 on v1

--- a/solution.py
+++ b/solution.py
@@ -32,14 +32,14 @@
 
 def kernel(
     sections, li_ref, og_ref, mod_ref, w_ref, out_ref, mg_ref,
-    og_all, li_all, w_all, st_all, scaled, normed, inv_all, modulated, gm, gn, outgoing,
-    gate_acc, sums, part, gate_buf, gate_rx, rs, full, send_sem, recv_sem, local_sem,
+    li_own, og_all, li_all, w_all, st_all, scaled, normed, inv_all, modulated, gm, gn, outgoing,
+    gate_acc, sums, part, part_rx, gate_buf, gate_rx, by_z, full, send_sem, recv_sem, local_sem,
 ):
     rows, feats = og_ref.shape
     block = feats // 4
     chunk = feats // 16
     w_rows = w_ref.shape[0]
-    owners = block // LANES
+    lot = block // 2
     half, w_half = rows // 2, w_rows // 2
 
     sec = lax.axis_index("section")
@@ -55,6 +55,9 @@
     def at_z(dz, dc):
         return (sec, x * 8 + lax.rem(z + dz, 4) * 2 + lax.rem(c + dc, 2))
 
+    def at_plane(k, dc):
+        return (sec, lax.rem(x + k, 4) * 8 + z * 2 + lax.rem(c + dc, 2))
+
     def at_section(step, pos):
         return (sec + step, pos * 8 + z * 2 + c)
 
@@ -66,7 +69,7 @@
 
     ids = iter(range(COPIES))
     slot_x = [lax.rem(x + OFF[n], 4) for n in range(4)]
-    group = [(dz, dc) for dz in range(4) for dc in range(2) if (dz, dc) != (0, 0)]
+    plane = [(k, dc) for k in range(4) for dc in range(2) if (k, dc) != (0, 0)]
 
     def columns(pos):
         return pl.ds(pl.multiple_of(pos * block, LANES), block)
@@ -78,10 +81,10 @@
     def greet(device):
         pl.semaphore_signal(barrier, inc=1, device_id=device, device_id_type=MESH)
 
-    for k in range(1, 4):
-        greet(at_x(k))
-    for dz, dc in group:
-        greet(at_z(dz, dc))
+    for k, dc in plane:
+        greet(at_plane(k, dc))
+    for dz in range(1, 4):
+        greet(at_z(dz, 0))
 
     @pl.when(sec > 0)
     def _():
@@ -94,7 +97,7 @@
             greet(at_section(1, pos))
 
     neighbours = (sec + sections - 1) // sections + (2 * sections - 2 - sec) // sections
-    pl.semaphore_wait(barrier, 3 + len(group) + 4 * neighbours)
+    pl.semaphore_wait(barrier, 3 + len(plane) + 4 * neighbours)
 
     low, high = pl.ds(0, half), pl.ds(half, half)
     w_low, w_high = pl.ds(0, w_half), pl.ds(w_half, w_half)
@@ -125,7 +128,7 @@
         step.start()
     local = [
         pltpu.make_async_copy(og_ref, og_all.at[0], local_sem.at[0]),
-        pltpu.make_async_copy(li_ref.at[:, own_columns], li_all.at[0], local_sem.at[1]),
+        pltpu.make_async_copy(li_ref, li_own, local_sem.at[1]),
         pltpu.make_async_copy(w_ref, w_all.at[0, c], local_sem.at[2]),
     ]
     for step in local:
@@ -141,7 +144,10 @@
         sib_sends.append(send)
         sib_waits.setdefault(slot, []).append(copy(ident, place, w_all.at[slot, other, part_rows], at_z(0, 1)))
 
-    values = li_ref[...].astype(F32)
+    for step in local:
+        step.wait()
+    li_all[0] = li_own[:, own_columns]
+    values = li_own[...].astype(F32)
     mean = jnp.sum(values, axis=1, keepdims=True) / feats
     center = values - mean
     variance = jnp.sum(center * center, axis=1, keepdims=True) / feats
@@ -149,8 +155,6 @@
     for step in st_sends:
         step.start()
     gate_acc[...] = jnp.zeros_like(gate_acc)
-    for step in local:
-        step.wait()
 
     def scale_grad(n):
         gate = mod_ref[2, pl.ds(slot_x[n], 1), :]
@@ -188,35 +192,26 @@
         li_sends[n - 1].wait_recv()
         st_sends[n - 1].wait_recv()
         modulate(n)
-    w_u_high.wait_recv()
-    to_sibling(1, w_high)
-    w_d_low.wait_recv()
-    to_sibling(2, w_low)
-    w_sib_in.wait_recv()
-    for slot in (1, 2):
-        for step in sib_waits[slot]:
-            step.wait_recv()
-
     tile = 512
 
     def chunk_of(slot):
-        return lax.rem(z + jnp.where(slot == 1, 3, jnp.where(slot == 2, 1, jnp.where(slot == 3, 2, 0))), 4)
+        return lax.rem(z + OFF[slot], 4)
 
     def grad_product(slot, first, count):
-        j = chunk_of(slot)
         left = scaled[first:first + count].reshape(count * rows, feats)
         right = w_all[slot].reshape(chunk, feats)
         product = lax.dot_general(left, right, (((1,), (1,)), ((), ())), preferred_element_type=F32)
-        gm[j, first:first + count] = product.reshape(count, rows, chunk)
-
-    def branch_product(slot, first, count):
-        j = chunk_of(slot)
-
+        gm[chunk_of(slot), first:first + count] = product.reshape(count, rows, chunk)
+
+    def branch_product(slots, first, count):
         def body(step, carry):
             cols = pl.ds(pl.multiple_of(step * tile, tile), tile)
-            left = modulated[j, first:first + count].reshape(count * rows, chunk)
-            right = w_all[slot, :, :, cols].reshape(chunk, tile)
-            branch = jnp.dot(left, right, preferred_element_type=F32)
+            branch = None
+            for slot in slots:
+                left = modulated[chunk_of(slot), first:first + count].reshape(count * rows, chunk)
+                right = w_all[slot, :, :, cols].reshape(chunk, tile)
+                term = jnp.dot(left, right, preferred_element_type=F32)
+                branch = term if branch is None else branch + term
             weighed = branch.reshape(count, rows, tile) * og_all[first:first + count, :, cols].astype(F32)
             gate_acc[first:first + count, :, cols] += jnp.sum(
                 weighed.reshape(count, rows // 8, 8, tile), axis=1
@@ -225,15 +220,18 @@
 
         lax.fori_loop(0, feats // tile, body, 0)
 
-    def early(first, count):
-        def body(slot, carry):
-            grad_product(slot, first, count)
-            branch_product(slot, first, count)
-            return carry
-
-        lax.fori_loop(0, 3, body, 0)
-
-    early(0, 3)
+    w_sib_in.wait_recv()
+    grad_product(0, 0, 3)
+    branch_product((0,), 0, 3)
+
+    w_u_high.wait_recv()
+    to_sibling(1, w_high)
+    w_d_low.wait_recv()
+    to_sibling(2, w_low)
+    for slot in (1, 2):
+        for step in sib_waits[slot]:
+            step.wait_recv()
+        grad_product(slot, 0, 3)
 
     og_fr.wait_recv()
     og_fl.wait_recv()
@@ -241,7 +239,10 @@
     li_sends[2].wait_recv()
     st_sends[2].wait_recv()
     modulate(3)
-    early(3, 1)
+    for slot in (0, 1, 2):
+        grad_product(slot, 3, 1)
+    branch_product((1, 2), 0, 3)
+    branch_product((0, 1, 2), 3, 1)
 
     w_fu.wait_recv()
     to_sibling(3, w_low)
@@ -273,6 +274,47 @@
             total = total + jnp.where(row == slot_x[n], per_slot[n], 0.0)
         return total
 
+    branch_product((3,), 0, 4)
+    gate_buf[...] = place_rows([jnp.sum(gate_acc[n], axis=0, keepdims=True) for n in range(4)])
+
+    def lot_of(pos, core):
+        return pl.ds(pl.multiple_of(pos * block + core * lot, LANES), lot)
+
+    gate_sends = [
+        copy(
+            next(ids), gate_buf.at[:, lot_of(lax.rem(x + k, 4), lax.rem(c + dc, 2))], gate_rx.at[i],
+            at_plane(k, dc),
+        )
+        for i, (k, dc) in enumerate(plane)
+    ]
+    for step in gate_sends:
+        step.start()
+
+    for step in sum_sends:
+        step.wait_recv()
+    hand_ids = [next(ids) for n in range(4)]
+
+    def hand(n):
+        return copy(hand_ids[n], outgoing.at[n], out_ref.at[:, own_columns], at_section(-1, slot_x[n]))
+
+    for n in range(4):
+        rows_of = sums[0, slot_x[n]] + sums[1, slot_x[n]] + sums[2, slot_x[n]] + sums[3, slot_x[n]]
+        first, second = rows_to_stats(rows_of)
+        centered = gn[n] - first / feats
+        grad_in = og_all[n, :, own_columns].astype(F32) + inv_all[n] * (centered - normed[n] * (second / feats))
+        outgoing[n] = grad_in.astype(BF16)
+
+        @pl.when(sec > 0)
+        def _(n=n):
+            hand(n).start()
+
+    zero_copy = pltpu.make_async_copy(scaled.at[0], out_ref, local_sem.at[3])
+
+    @pl.when(sec == sections - 1)
+    def _():
+        scaled[0] = jnp.zeros_like(scaled[0])
+        zero_copy.start()
+
     shifts, scales = [], []
     for n in range(4):
         grad_mod = joined(n)
@@ -281,111 +323,45 @@
     part[0] = place_rows(shifts)
     part[1] = place_rows(scales)
 
-    for step in sum_sends:
-        step.wait_recv()
-    hand_ids = [next(ids) for n in range(4)]
-
-    def hand(n):
-        return copy(hand_ids[n], outgoing.at[n], out_ref.at[:, own_columns], at_section(-1, slot_x[n]))
-
-    for n in range(4):
-        rows_of = sums[0, slot_x[n]] + sums[1, slot_x[n]] + sums[2, slot_x[n]] + sums[3, slot_x[n]]
-        first, second = rows_to_stats(rows_of)
-        centered = gn[n] - first / feats
-        grad_in = og_all[n, :, own_columns].astype(F32) + inv_all[n] * (centered - normed[n] * (second / feats))
-        outgoing[n] = grad_in.astype(BF16)
-
-        @pl.when(sec > 0)
-        def _(n=n):
-            hand(n).start()
-
-    @pl.when(sec == sections - 1)
-    def _():
-        out_ref[...] = jnp.zeros_like(out_ref)
-
-    branch_product(3, 0, 4)
-
-    gate_buf[...] = place_rows([jnp.sum(gate_acc[n], axis=0, keepdims=True) for n in range(4)])
-    gate_sends = [
-        copy(next(ids), gate_buf.at[:, columns(lax.rem(x + AWAY[n], 4))], gate_rx.at[n - 1], at_x(AWAY[n]))
-        for n in (1, 2, 3)
-    ]
-    for step in gate_sends:
-        step.start()
+    part_send = copy(next(ids), part.at[:, :, lot_of(0, other)], part_rx, at_z(0, 1))
+    part_send.start()
     for step in gate_sends:
         step.wait_recv()
-    part[2] = gate_buf[:, own_columns] + gate_rx[0] + gate_rx[1] + gate_rx[2]
-
-    def owned(owner):
-        return pl.ds(pl.multiple_of(owner * LANES, LANES), LANES)
-
-    owns = z < owners // 2
-    me = z * 2 + c
-    rs_ids = [next(ids) for _ in group]
-    ag_ids = [next(ids) for _ in group]
-
-    def rs_copy(i):
-        dz, dc = group[i]
-        owner = lax.rem(z + dz, 4) * 2 + lax.rem(c + dc, 2)
-        return copy(rs_ids[i], part.at[:, :, owned(owner)], rs.at[i], at_z(dz, dc))
-
-    def gives(i):
-        return lax.rem(z + group[i][0], 4) < owners // 2
-
-    for i in range(len(group)):
-        @pl.when(gives(i))
-        def _(i=i):
-            rs_copy(i).start()
-
-    @pl.when(owns)
-    def _():
-        total = part[:, :, owned(me)]
-        for i in range(len(group)):
-            dz, dc = group[i]
-            copy(rs_ids[i], rs.at[i], rs.at[i], at_z(dz, dc)).wait_recv()
-        for i in range(len(group)):
-            total = total + rs[i]
-        full[0, me] = total
-        for i in range(len(group)):
-            dz, dc = group[i]
-            copy(ag_ids[i], full.at[0, me], full.at[0, me], at_z(dz, dc)).start()
-
-    for i in range(len(group)):
-        dz, dc = group[i]
-        from_z = lax.rem(z + 4 - dz, 4)
-        source = from_z * 2 + lax.rem(c + dc, 2)
-
-        @pl.when(from_z < owners // 2)
-        def _(i=i, source=source, dz=dz, dc=dc):
-            landed = full.at[0, source]
-            copy(ag_ids[i], landed, landed, at_z(dz, dc)).wait_recv()
-
-    full_sends = [copy(next(ids), full.at[0], full.at[n], at_x(AWAY[n])) for n in (1, 2, 3)]
+    gate = gate_buf[:, lot_of(x, c)]
+    for i in range(len(plane)):
+        gate = gate + gate_rx[i]
+    by_z[z, 2] = gate
+    part_send.wait_recv()
+    by_z[z, 0:2] = part[:, :, lot_of(0, c)] + part_rx[...]
+    z_ids = [next(ids) for _ in range(3)]
+    z_sends = []
+    for i in range(3):
+        held = by_z.at[lax.rem(z + 4 - i, 4)]
+        step = copy(z_ids[i], held, held, at_z(1, 0))
+        step.start()
+        z_sends.append(step)
+        landed = by_z.at[lax.rem(z + 3 - i, 4)]
+        copy(z_ids[i], landed, landed, at_z(1, 0)).wait_recv()
+    full[x, c] = by_z[0] + by_z[1] + by_z[2] + by_z[3]
+    full_ids = [next(ids) for _ in plane]
+    full_sends = [
+        copy(full_ids[i], full.at[x, c], full.at[x, c], at_plane(k, dc)) for i, (k, dc) in enumerate(plane)
+    ]
     for step in full_sends:
         step.start()
-    for step in full_sends:
-        step.wait_recv()
-    for n in range(4):
-        for owner in range(owners):
-            start = pl.multiple_of(slot_x[n] * block + owner * LANES, LANES)
-            mg_ref[:, :, pl.ds(start, LANES)] = full[n, owner]
+    for i, (k, dc) in enumerate(plane):
+        landed = full.at[lax.rem(x + 4 - k, 4), lax.rem(c + dc, 2)]
+        copy(full_ids[i], landed, landed, at_plane(k, dc)).wait_recv()
+    for pos in range(4):
+        for core in range(2):
+            start = pos * block + core * lot
+            mg_ref[:, :, start:start + lot] = full[pos, core]
 
     for step in (
         og_r_low, og_r_high, og_l_high, og_l_low, og_fr, og_fl, w_u_low, w_u_high, w_d_high, w_d_low,
-        w_fu, w_fd, *li_sends, *st_sends, *sib_sends, *sum_sends, *gate_sends, *full_sends,
+        w_fu, w_fd, *li_sends, *st_sends, *sib_sends, *sum_sends, *gate_sends, part_send, *z_sends, *full_sends,
     ):
         step.wait_send()
-    for i in range(len(group)):
-        @pl.when(gives(i))
-        def _(i=i):
-            rs_copy(i).wait_send()
-
-    @pl.when(owns)
-    def _():
-        for i in range(len(group)):
-            dz, dc = group[i]
-            copy(ag_ids[i], full.at[0, me], full.at[0, me], at_z(dz, dc)).wait_send()
-
     @pl.when(sec > 0)
     def _():
         for n in range(4):
@@ -396,6 +372,10 @@
         for n in range(4):
             landed = out_ref.at[:, columns(lax.rem(x + 4 - OFF[n], 4))]
             copy(hand_ids[n], outgoing.at[n], landed, at_section(1, slot_x[n])).wait_recv()
+
+    @pl.when(sec == sections - 1)
+    def _():
+        zero_copy.wait()
 
 
 def on_device(layer_input, out_grad, modulation, proj_weight):
@@ -403,17 +383,19 @@
     rows, feats = layer_input.shape[1:]
     w_rows = proj_weight.shape[1]
     block, chunk = feats // 4, feats // 16
-    owners = block // LANES
+    lot = block // 2
     vmem = pl.BlockSpec(memory_space=pltpu.VMEM)
+    anywhere = pl.BlockSpec(memory_space=pl.ANY)
     handoff, grads = pl.pallas_call(
         functools.partial(kernel, sections),
         out_shape=(
             jax.ShapeDtypeStruct((rows, feats), BF16),
             jax.ShapeDtypeStruct((3, SEQS, feats), F32),
         ),
-        in_specs=[vmem] * 4,
-        out_specs=(vmem, vmem),
+        in_specs=[anywhere, anywhere, vmem, anywhere],
+        out_specs=(anywhere, vmem),
         scratch_shapes=[
+            pltpu.VMEM((rows, feats), BF16),
             pltpu.VMEM((4, rows, feats), BF16),
             pltpu.VMEM((4, rows, block), BF16),
             pltpu.VMEM((4, 2, w_rows, feats), BF16),
@@ -427,14 +409,15 @@
             pltpu.VMEM((4, rows, block), BF16),
             pltpu.VMEM((4, 8, feats), F32),
             pltpu.VMEM((4, 4, 8, LANES), F32),
-            pltpu.VMEM((3, SEQS, block), F32),
+            pltpu.VMEM((2, SEQS, block), F32),
+            pltpu.VMEM((2, SEQS, lot), F32),
             pltpu.VMEM((SEQS, feats), F32),
-            pltpu.VMEM((3, SEQS, block), F32),
-            pltpu.VMEM((7, 3, SEQS, LANES), F32),
-            pltpu.VMEM((4, owners, 3, SEQS, LANES), F32),
+            pltpu.VMEM((7, SEQS, lot), F32),
+            pltpu.VMEM((4, 3, SEQS, lot), F32),
+            pltpu.VMEM((4, 2, 3, SEQS, lot), F32),
             pltpu.SemaphoreType.DMA((COPIES,)),
             pltpu.SemaphoreType.DMA((COPIES,)),
-            pltpu.SemaphoreType.DMA((3,)),
+            pltpu.SemaphoreType.DMA((4,)),
         ],
         compiler_params=pltpu.CompilerParams(
             collective_id=0, has_side_effects=True, vmem_limit_bytes=56 * 1024 * 1024

time: 103 us -> 90.4 us (0.88)
  the two profiles are of different devices: /device:TPU:120 before, /device:TPU:57 now
where the time goes in v2:
time: 90.4 us; the launch traced here: 89.5 us
  Pallas kernels  86.1 us (95%)
  local copies, waits for them, and re-layouts  2.76 us (3%)
    pallas_call x1, Pallas kernels, on_device(): pl.pallas_call(functools.partial(kernel, sections), out_shape=(jax.ShapeD...  86.1 us
    unnamed x4, local copies, waits for them, and re-layouts  2.76 us

profile of v2, /device:TPU:57, one launch (start us, length us, event | category | flops | bytes accessed | tf_op | source)
XLA Modules:
  0.0 89.5 jit_solution(17047719415374993349)
XLA Ops:
  0.6 86.1 %shard_map.59 = (bf16[128,3072]{1,0:T(8,128)(2,1)}, f32[3,4,3072]{2,1,0:T(4,128)}) custom-call(bf16[128,3072]{1,0:T(8,128)(2,1)} %bitcast.11, bf16[128,3072]{1,0:T(8,128)(2,1)} %bitcast.12, f32[3,4,3072]{2,1,0:T(4,128)} %bitcast.14, bf16[96,3072]{1,0:T(8,128)(2,1)} %bitcast.13), custom_call_target="tpu_custom_call" | custom-call | tf_op jit(solution)/shard_map/pallas_call | solution.py:389
  86.7 0.0 copy-start
  86.7 2.1 %copy.8 = bf16[1,128,3072]{2,1,0:T(8,128)(2,1)} copy(bf16[1,128,3072]{2,1,0:T(8,128)(2,1)} %bitcast.10) | data formatting | bytes 1572864
  88.8 0.0 copy-done
  88.8 0.7 copy.9
Async XLA Ops:
  86.7 2.1 %copy-start = (f32[3,4,3072]{2,1,0:T(4,128)S(1)}, f32[3,4,3072]{2,1,0:T(4,128)}, u32[]{:S(2)}) copy-start(f32[3,4,3072]{2,1,0:T(4,128)} %get-tuple-element.5) | copy-start | bytes 442372

commit v3 on v2

--- a/solution.py
+++ b/solution.py
@@ -15,7 +15,7 @@
 OFF = (0, 3, 1, 2)
 AWAY = (0, 1, 3, 2)
 LANES = 128
-COPIES = 64
+COPIES = 96
 
 
 def stats_to_rows(first, second):
@@ -32,8 +32,9 @@
 
 def kernel(
     sections, li_ref, og_ref, mod_ref, w_ref, out_ref, mg_ref,
-    li_own, og_all, li_all, w_all, st_all, scaled, normed, inv_all, modulated, gm, gn, outgoing,
-    gate_acc, sums, part, part_rx, gate_buf, gate_rx, by_z, full, send_sem, recv_sem, local_sem,
+    li_own, og_all, li_all, w_all, st_all, scaled, normed, inv_all, modulated, gm, norm_by, first_sum, second_sum, outgoing,
+    gate_acc, sums, part, part_rx, gate_buf, gate_rx, by_z, full, factor, chunk_tx, chunk_rx,
+    next_li, next_og, mean_tx, mean_rx, ready, relay, send_sem, recv_sem, local_sem,
 ):
     rows, feats = og_ref.shape
     block = feats // 4
@@ -67,6 +68,10 @@
             device_id=device, device_id_type=MESH,
         )
 
+    corner = sections // 2
+    streams = jnp.logical_and(sec > 0, sec != corner)
+    hears = jnp.logical_and(sec < sections - 1, sec != corner - 1)
+
     ids = iter(range(COPIES))
     slot_x = [lax.rem(x + OFF[n], 4) for n in range(4)]
     plane = [(k, dc) for k in range(4) for dc in range(2) if (k, dc) != (0, 0)]
@@ -96,8 +101,27 @@
         for pos in range(4):
             greet(at_section(1, pos))
 
+    @pl.when(sec == corner)
+    def _():
+        for pos in range(4):
+            greet(at_section(-corner, pos))
+
+    @pl.when(sec == 0)
+    def _():
+        for pos in range(4):
+            greet(at_section(corner, pos))
+        greet(at_section(corner - 1, x))
+
+    @pl.when(sec == corner - 1)
+    def _():
+        greet(at_section(1 - corner, x))
+
+    def one_if(test):
+        return jnp.where(test, 1, 0)
+
+    extra = 4 * one_if(sec == corner) + 5 * one_if(sec == 0) + one_if(sec == corner - 1)
     neighbours = (sec + sections - 1) // sections + (2 * sections - 2 - sec) // sections
-    pl.semaphore_wait(barrier, 3 + len(plane) + 4 * neighbours)
+    pl.semaphore_wait(barrier, 3 + len(plane) + 4 * neighbours + extra)
 
     low, high = pl.ds(0, half), pl.ds(half, half)
     w_low, w_high = pl.ds(0, w_half), pl.ds(w_half, w_half)
@@ -126,6 +150,14 @@
         step.start()
     for step in li_sends:
         step.start()
+    og_next = copy(next(ids), og_ref, next_og, at_section(-1, x))
+    li_next = copy(next(ids), li_ref, next_li, at_section(-1, x))
+
+    @pl.when(streams)
+    def _():
+        li_next.start()
+        og_next.start()
+
     local = [
         pltpu.make_async_copy(og_ref, og_all.at[0], local_sem.at[0]),
         pltpu.make_async_copy(li_ref, li_own, local_sem.at[1]),
@@ -170,6 +202,8 @@
         mod_n = (norm_n * (1.0 + scale) + shift).astype(BF16)
         for j in range(4):
             modulated[j, n] = mod_n[:, j * chunk:(j + 1) * chunk]
+            factor[j, n] = 1.0 + scale[:, j * chunk:(j + 1) * chunk]
+            norm_by[j, n] = norm_n[:, j * chunk:(j + 1) * chunk]
 
     scale_grad(0)
     modulate(0)
@@ -197,11 +231,40 @@
     def chunk_of(slot):
         return lax.rem(z + OFF[slot], 4)
 
+    sum_sends = [copy(next(ids), sums.at[0], sums.at[n], at_x(AWAY[n])) for n in (1, 2, 3)]
+    chunk_ids = [[next(ids) for n in range(4)] for slot in range(4)]
+
+    def chunk_copy(slot, n):
+        j = chunk_of(slot)
+        return copy(chunk_ids[slot][n], chunk_tx.at[n, j], chunk_rx.at[n, j], at_section(-1, slot_x[n]))
+
     def grad_product(slot, first, count):
         left = scaled[first:first + count].reshape(count * rows, feats)
         right = w_all[slot].reshape(chunk, feats)
         product = lax.dot_general(left, right, (((1,), (1,)), ((), ())), preferred_element_type=F32)
         gm[chunk_of(slot), first:first + count] = product.reshape(count, rows, chunk)
+        for n in range(first, first + count):
+            grad_norm = gm[chunk_of(slot), n] * factor[chunk_of(slot), n]
+            one = jnp.sum(grad_norm, axis=1, keepdims=True)
+            two = jnp.sum(grad_norm * norm_by[chunk_of(slot), n], axis=1, keepdims=True)
+            if slot == 3:
+                sums[0, slot_x[n]] = stats_to_rows(first_sum[n] + one, second_sum[n] + two)
+            elif slot == 0:
+                first_sum[n] = one
+                second_sum[n] = two
+            else:
+                first_sum[n] += one
+                second_sum[n] += two
+        if slot == 3:
+            for step in sum_sends:
+                step.start()
+
+        @pl.when(streams)
+        def _():
+            for n in range(first, first + count):
+                term = inv_all[n] * (gm[chunk_of(slot), n] * factor[chunk_of(slot), n])
+                chunk_tx[n, chunk_of(slot)] = term.astype(BF16)
+                chunk_copy(slot, n).start()
 
     def branch_product(slots, first, count):
         def body(step, carry):
@@ -255,18 +318,6 @@
     def joined(n):
         return jnp.concatenate([gm[j, n] for j in range(4)], axis=1)
 
-    for n in range(4):
-        scale = mod_ref[1, pl.ds(slot_x[n], 1), own_columns]
-        grad_norm = joined(n) * (1.0 + scale)
-        gn[n] = grad_norm
-        sums[0, slot_x[n]] = stats_to_rows(
-            jnp.sum(grad_norm, axis=1, keepdims=True),
-            jnp.sum(grad_norm * normed[n], axis=1, keepdims=True),
-        )
-    sum_sends = [copy(next(ids), sums.at[0], sums.at[n], at_x(AWAY[n])) for n in (1, 2, 3)]
-    for step in sum_sends:
-        step.start()
-
     def place_rows(per_slot):
         row = lax.broadcasted_iota(jnp.int32, (SEQS, per_slot[0].shape[1]), 0)
         total = jnp.zeros(row.shape, F32)
@@ -275,8 +326,6 @@
         return total
 
     branch_product((3,), 0, 4)
-    gate_buf[...] = place_rows([jnp.sum(gate_acc[n], axis=0, keepdims=True) for n in range(4)])
-
     def lot_of(pos, core):
         return pl.ds(pl.multiple_of(pos * block + core * lot, LANES), lot)
 
@@ -287,26 +336,65 @@
         )
         for i, (k, dc) in enumerate(plane)
     ]
-    for step in gate_sends:
-        step.start()
+    def send_gates():
+        gate_buf[...] = place_rows([jnp.sum(gate_acc[n], axis=0, keepdims=True) for n in range(4)])
+        for step in gate_sends:
+            step.start()
+
+    pl.when(sec != corner)(send_gates)
 
     for step in sum_sends:
         step.wait_recv()
+    def row_means(n):
+        rows_of = sums[0, slot_x[n]] + sums[1, slot_x[n]] + sums[2, slot_x[n]] + sums[3, slot_x[n]]
+        return rows_of
+
+    mean_tx[...] = row_means(0)
+    mean_send = copy(next(ids), mean_tx, mean_rx, at_section(-1, x))
+
+    @pl.when(streams)
+    def _():
+        mean_send.start()
+
     hand_ids = [next(ids) for n in range(4)]
 
     def hand(n):
-        return copy(hand_ids[n], outgoing.at[n], out_ref.at[:, own_columns], at_section(-1, slot_x[n]))
-
-    for n in range(4):
-        rows_of = sums[0, slot_x[n]] + sums[1, slot_x[n]] + sums[2, slot_x[n]] + sums[3, slot_x[n]]
-        first, second = rows_to_stats(rows_of)
-        centered = gn[n] - first / feats
-        grad_in = og_all[n, :, own_columns].astype(F32) + inv_all[n] * (centered - normed[n] * (second / feats))
-        outgoing[n] = grad_in.astype(BF16)
-
-        @pl.when(sec > 0)
-        def _(n=n):
+        return copy(hand_ids[n], outgoing.at[n, straight], out_ref.at[straight, own_columns], at_section(-1, slot_x[n]))
+
+    via_ids = [next(ids) for n in range(4)]
+    relay_ids = [next(ids) for n in range(4)]
+    straight, around = pl.ds(0, rows - relay.shape[1]), pl.ds(rows - relay.shape[1], relay.shape[1])
+
+    def via(n):
+        return copy(via_ids[n], outgoing.at[n, around], relay.at[n], at_section(-corner, slot_x[n]))
+
+    def from_columns(n):
+        return columns(lax.rem(x + 4 - OFF[n], 4))
+
+    def relayed(n):
+        return copy(relay_ids[n], relay.at[n], out_ref.at[around, from_columns(n)], at_section(corner - 1, x))
+
+    def pass_on(*which):
+        @pl.when(sec == 0)
+        def _():
+            for n in which:
+                copy(via_ids[n], relay.at[n], relay.at[n], at_section(corner, slot_x[n])).wait_recv()
+                relayed(n).start()
+
+    @pl.when(sec == corner)
+    def _():
+        for n in range(4):
+            first, second = rows_to_stats(row_means(n))
+            scale = mod_ref[1, pl.ds(slot_x[n], 1), own_columns]
+            centered = joined(n) * (1.0 + scale) - first / feats
+            grad_in = og_all[n, :, own_columns].astype(F32) + inv_all[n] * (
+                centered - normed[n] * (second / feats)
+            )
+            outgoing[n] = grad_in.astype(BF16)
+            via(n).start()
             hand(n).start()
+
+    pl.when(sec == corner)(send_gates)
 
     zero_copy = pltpu.make_async_copy(scaled.at[0], out_ref, local_sem.at[3])
 
@@ -333,15 +421,32 @@
     by_z[z, 2] = gate
     part_send.wait_recv()
     by_z[z, 0:2] = part[:, :, lot_of(0, c)] + part_rx[...]
-    z_ids = [next(ids) for _ in range(3)]
-    z_sends = []
-    for i in range(3):
+    z_ids = [next(ids) for _ in range(6)]
+    edge_plane = lax.rem(sec, corner) == corner - 1
+
+    def round_z(i):
         held = by_z.at[lax.rem(z + 4 - i, 4)]
-        step = copy(z_ids[i], held, held, at_z(1, 0))
-        step.start()
-        z_sends.append(step)
-        landed = by_z.at[lax.rem(z + 3 - i, 4)]
-        copy(z_ids[i], landed, landed, at_z(1, 0)).wait_recv()
+        return copy(z_ids[i], held, held, at_z(1, 0))
+
+    def across_z(i):
+        return copy(z_ids[3 + i], by_z.at[z], by_z.at[z], at_z(i + 1, 0))
+
+    @pl.when(edge_plane)
+    def _():
+        for i in range(3):
+            round_z(i).start()
+            landed = by_z.at[lax.rem(z + 3 - i, 4)]
+            copy(z_ids[i], landed, landed, at_z(1, 0)).wait_recv()
+
+    @pl.when(jnp.logical_not(edge_plane))
+    def _():
+        for i in range(3):
+            across_z(i).start()
+        pass_on(0)
+        for i in range(3):
+            landed = by_z.at[lax.rem(z + 3 - i, 4)]
+            copy(z_ids[3 + i], landed, landed, at_z(i + 1, 0)).wait_recv()
+
     full[x, c] = by_z[0] + by_z[1] + by_z[2] + by_z[3]
     full_ids = [next(ids) for _ in plane]
     full_sends = [
@@ -349,6 +454,32 @@
     ]
     for step in full_sends:
         step.start()
+    pass_on(1, 2)
+
+    def finished(n):
+        return pltpu.make_async_copy(ready.at[n], out_ref.at[:, from_columns(n)], local_sem.at[4 + n])
+
+    @pl.when(hears)
+    def _():
+        li_next.wait_recv()
+        later = next_li[...].astype(F32)
+        later_mean = jnp.sum(later, axis=1, keepdims=True) / feats
+        later_center = later - later_mean
+        later_inv = lax.rsqrt(jnp.sum(later_center * later_center, axis=1, keepdims=True) / feats + 1e-06)
+        og_next.wait_recv()
+        mean_send.wait_recv()
+        first, second = rows_to_stats(mean_rx[...])
+        for n in range(4):
+            for slot in range(4):
+                chunk_copy(slot, n).wait_recv()
+            cols = from_columns(n)
+            term = jnp.concatenate([chunk_rx[n, j].astype(F32) for j in range(4)], axis=1)
+            norm_n = (next_li[:, cols].astype(F32) - later_mean) * later_inv
+            taken = later_inv * (first / feats + norm_n * (second / feats))
+            ready[n] = (next_og[:, cols].astype(F32) + (term - taken)).astype(BF16)
+            finished(n).start()
+
+    pass_on(3)
     for i, (k, dc) in enumerate(plane):
         landed = full.at[lax.rem(x + 4 - k, 4), lax.rem(c + dc, 2)]
         copy(full_ids[i], landed, landed, at_plane(k, dc)).wait_recv()
@@ -359,19 +490,51 @@
 
     for step in (
         og_r_low, og_r_high, og_l_high, og_l_low, og_fr, og_fl, w_u_low, w_u_high, w_d_high, w_d_low,
-        w_fu, w_fd, *li_sends, *st_sends, *sib_sends, *sum_sends, *gate_sends, part_send, *z_sends, *full_sends,
+        w_fu, w_fd, *li_sends, *st_sends, *sib_sends, *sum_sends, *gate_sends, part_send, *full_sends,
     ):
         step.wait_send()
-    @pl.when(sec > 0)
+    @pl.when(edge_plane)
+    def _():
+        for i in range(3):
+            round_z(i).wait_send()
+
+    @pl.when(jnp.logical_not(edge_plane))
+    def _():
+        for i in range(3):
+            across_z(i).wait_send()
+
+    @pl.when(streams)
+    def _():
+        og_next.wait_send()
+        li_next.wait_send()
+        mean_send.wait_send()
+        for slot in range(4):
+            for n in range(4):
+                chunk_copy(slot, n).wait_send()
+
+    @pl.when(hears)
+    def _():
+        for n in range(4):
+            finished(n).wait()
+
+    @pl.when(sec == corner)
     def _():
         for n in range(4):
             hand(n).wait_send()
-
-    @pl.when(sec < sections - 1)
+            via(n).wait_send()
+
+    @pl.when(sec == 0)
     def _():
         for n in range(4):
-            landed = out_ref.at[:, columns(lax.rem(x + 4 - OFF[n], 4))]
-            copy(hand_ids[n], outgoing.at[n], landed, at_section(1, slot_x[n])).wait_recv()
+            relayed(n).wait_send()
+
+    @pl.when(sec == corner - 1)
+    def _():
+        for n in range(4):
+            landed = out_ref.at[straight, from_columns(n)]
+            copy(hand_ids[n], outgoing.at[n, straight], landed, at_section(1, slot_x[n])).wait_recv()
+            landed = out_ref.at[around, from_columns(n)]
+            copy(relay_ids[n], relay.at[n], landed, at_section(1 - corner, x)).wait_recv()
 
     @pl.when(sec == sections - 1)
     def _():
@@ -405,7 +568,9 @@
             pltpu.VMEM((4, rows, 1), F32),
             pltpu.VMEM((4, 4, rows, chunk), BF16),
             pltpu.VMEM((4, 4, rows, chunk), F32),
-            pltpu.VMEM((4, rows, block), F32),
+            pltpu.VMEM((4, 4, rows, chunk), F32),
+            pltpu.VMEM((4, rows, 1), F32),
+            pltpu.VMEM((4, rows, 1), F32),
             pltpu.VMEM((4, rows, block), BF16),
             pltpu.VMEM((4, 8, feats), F32),
             pltpu.VMEM((4, 4, 8, LANES), F32),
@@ -415,14 +580,25 @@
             pltpu.VMEM((7, SEQS, lot), F32),
             pltpu.VMEM((4, 3, SEQS, lot), F32),
             pltpu.VMEM((4, 2, 3, SEQS, lot), F32),
+            pltpu.VMEM((4, 4, 1, chunk), F32),
+            pltpu.VMEM((4, 4, rows, chunk), BF16),
+            pltpu.VMEM((4, 4, rows, chunk), BF16),
+            pltpu.VMEM((rows, feats), BF16),
+            pltpu.VMEM((rows, feats), BF16),
+            pltpu.VMEM((8, LANES), F32),
+            pltpu.VMEM((8, LANES), F32),
+            pltpu.VMEM((4, rows, block), BF16),
+            pltpu.VMEM((4, rows * 3 // 8, block), BF16),
             pltpu.SemaphoreType.DMA((COPIES,)),
             pltpu.SemaphoreType.DMA((COPIES,)),
-            pltpu.SemaphoreType.DMA((4,)),
+            pltpu.SemaphoreType.DMA((8,)),
         ],
         compiler_params=pltpu.CompilerParams(
             collective_id=0, has_side_effects=True, vmem_limit_bytes=56 * 1024 * 1024
         ),
     )(layer_input[0], out_grad[0], jnp.transpose(modulation[0], (1, 0, 2)), proj_weight[0])
+    last = lax.axis_index("section") == sections - 1
+    handoff = jnp.where(last, jnp.zeros_like(handoff), handoff)
     return (handoff[None], jnp.transpose(grads, (1, 0, 2))[None])
 
 

time: 90.4 us -> 88.3 us (0.977)
  other arithmetic: 0 us -> 2.11 us
  local copies, waits for them, and re-layouts: 2.76 us -> 0.67 us
  Pallas kernels: 86.1 us -> 84.7 us
    broadcast_in_dim x0 -> x1, other arithmetic: none -> 2.11 us  [on_device(): return (handoff[None], jnp.transpose(grads, (1, 0, 2))[None])]
    unnamed x4 -> x3, local copies, waits for them, and re-layouts: 2.76 us -> 0.67 us
    pallas_call x1, Pallas kernels: 86.1 us -> 84.7 us  [on_device(): pl.pallas_call(functools.partial(kernel, sections), out_shape=(jax.ShapeD...]
where the time goes in v3:
time: 88.3 us; the launch traced here: 88.2 us
  Pallas kernels  84.7 us (96%)
  other arithmetic  2.11 us (2%)
    pallas_call x1, Pallas kernels, on_device(): pl.pallas_call(functools.partial(kernel, sections), out_shape=(jax.ShapeD...  84.7 us
    broadcast_in_dim x1, other arithmetic, on_device(): return (handoff[None], jnp.transpose(grads, (1, 0, 2))[None])  2.11 us

profile of v3, /device:TPU:57, one launch (start us, length us, event | category | flops | bytes accessed | tf_op | source)
XLA Modules:
  0.0 88.2 jit_solution(11918050618381755614)
XLA Ops:
  0.6 84.7 %shard_map.59 = (bf16[128,3072]{1,0:T(8,128)(2,1)}, f32[3,4,3072]{2,1,0:T(4,128)}) custom-call(bf16[128,3072]{1,0:T(8,128)(2,1)} %bitcast.11, bf16[128,3072]{1,0:T(8,128)(2,1)} %bitcast.12, f32[3,4,3072]{2,1,0:T(4,128)} %bitcast.14, bf16[96,3072]{1,0:T(8,128)(2,1)} %bitcast.13), custom_call_target="tpu_custom_call" | custom-call | tf_op jit(solution)/shard_map/pallas_call | solution.py:552
  85.4 0.0 copy-start
  85.4 2.1 %select_bitcast_fusion = bf16[1,128,3072]{2,1,0:T(8,128)(2,1)} fusion(bf16[128,3072]{1,0:T(8,128)(2,1)} %get-tuple-element.4, pred[]{:T(512)S(6)} %eq.3), kind=kLoop, calls=%fused_computation | loop fusion | flops 393216 | bytes 1572865 | tf_op jit(solution)/shard_map/broadcast_in_dim | solution.py:602
  87.5 0.0 copy-done
  87.5 0.7 copy.7
Async XLA Ops:
  85.4 2.1 %copy-start = (f32[3,4,3072]{2,1,0:T(4,128)S(1)}, f32[3,4,3072]{2,1,0:T(4,128)}, u32[]{:S(2)}) copy-start(f32[3,4,3072]{2,1,0:T(4,128)} %get-tuple-element.5) | copy-start | bytes 442372

commit v4 on v3

--- a/solution.py
+++ b/solution.py
@@ -594,7 +594,7 @@
             pltpu.SemaphoreType.DMA((8,)),
         ],
         compiler_params=pltpu.CompilerParams(
-            collective_id=0, has_side_effects=True, vmem_limit_bytes=56 * 1024 * 1024
+            collective_id=0, has_side_effects=True, vmem_limit_bytes=52 * 1024 * 1024
         ),
     )(layer_input[0], out_grad[0], jnp.transpose(modulation[0], (1, 0, 2)), proj_weight[0])
     last = lax.axis_index("section") == sections - 1

time: 88.3 us -> 87.5 us (level)
  local copies, waits for them, and re-layouts: 0.67 us -> 2.63 us
  Pallas kernels: 84.7 us -> 83.1 us
  other arithmetic: 2.11 us -> 0.94 us
    unnamed x3 -> x5, local copies, waits for them, and re-layouts: 0.67 us -> 2.63 us
    pallas_call x1, Pallas kernels: 84.7 us -> 83.1 us  [on_device(): pl.pallas_call(functools.partial(kernel, sections), out_shape=(jax.ShapeD...]
    broadcast_in_dim x1, other arithmetic: 2.11 us -> 0.94 us  [on_device(): return (handoff[None], jnp.transpose(grads, (1, 0, 2))[None])]
where the time goes in v4:
time: 87.5 us; the launch traced here: 87.3 us
  Pallas kernels  83.1 us (95%)
  local copies, waits for them, and re-layouts  2.63 us (3%)
  other arithmetic  0.94 us (1%)
    pallas_call x1, Pallas kernels, on_device(): pl.pallas_call(functools.partial(kernel, sections), out_shape=(jax.ShapeD...  83.1 us
    unnamed x5, local copies, waits for them, and re-layouts  2.63 us

profile of v4, /device:TPU:57, one launch (start us, length us, event | category | flops | bytes accessed | tf_op | source)
XLA Modules:
  0.0 87.3 jit_solution(1158130569538366195)
XLA Ops:
  0.6 0.0 copy-start
  0.6 1.1 %copy-done = bf16[1,96,3072]{2,1,0:T(8,128)(2,1)S(1)} copy-done((bf16[1,96,3072]{2,1,0:T(8,128)(2,1)S(1)}, bf16[1,96,3072]{2,1,0:T(8,128)(2,1)}, u32[]{:S(2)}) %copy-start) | copy-done | bytes 589848
  1.7 0.0 copy-start.1
  1.7 0.9 %copy-done.1 = f32[1,4,3,3072]{3,1,2,0:T(4,128)S(1)} copy-done((f32[1,4,3,3072]{3,1,2,0:T(4,128)S(1)}, f32[1,4,3,3072]{3,1,2,0:T(4,128)}, u32[]{:S(2)}) %copy-start.1) | copy-done | bytes 147480
  2.6 83.1 %shard_map.59 = (bf16[128,3072]{1,0:T(8,128)(2,1)S(1)}, f32[3,4,3072]{2,1,0:T(4,128)S(1)}) custom-call(bf16[128,3072]{1,0:T(8,128)(2,1)} %bitcast.14, bf16[128,3072]{1,0:T(8,128)(2,1)} %bitcast.15, f32[3,4,3072]{2,1,0:T(4,128)S(1)} %bitcast.12, bf16[96,3072]{1,0:T(8,128)(2,1)S(1)} %bitcast.11), custom_call_target="tpu_custom_call" | custom-call | tf_op jit(solution)/shard_map/pallas_call | solution.py:552
  85.7 0.9 %select_bitcast_fusion = bf16[1,128,3072]{2,1,0:T(8,128)(2,1)} fusion(bf16[128,3072]{1,0:T(8,128)(2,1)S(1)} %get-tuple-element.4, pred[]{:T(512)S(6)} %eq.3), kind=kLoop, calls=%fused_computation | loop fusion | flops 393216 | bytes 1572865 | tf_op jit(solution)/shard_map/broadcast_in_dim | solution.py:602
  86.6 0.7 copy.7
Async XLA Ops:
  0.6 1.1 %copy-start = (bf16[1,96,3072]{2,1,0:T(8,128)(2,1)S(1)}, bf16[1,96,3072]{2,1,0:T(8,128)(2,1)}, u32[]{:S(2)}) copy-start(bf16[1,96,3072]{2,1,0:T(8,128)(2,1)} %param.7) | copy-start | bytes 1769476
  1.7 0.9 %copy-start.1 = (f32[1,4,3,3072]{3,1,2,0:T(4,128)S(1)}, f32[1,4,3,3072]{3,1,2,0:T(4,128)}, u32[]{:S(2)}) copy-start(f32[1,4,3,3072]{3,1,2,0:T(4,128)} %param.6) | copy-start | bytes 442372
